TPU v7x, 32 devices: a whole 2x2x4 slice. The times are simulated.
32 devices in a mesh: narrow: 4 (over y, x), wide: 8 (over z, core).
Axes of the slice: x: 2, y: 2, z: 4, core: 2. Of those that a mesh axis runs over, the one named last changes fastest.
Arguments:
- tokens: bfloat16 [32768, 768], P(('narrow', 'wide')), may hold values from -6 to 6
- frame_counts: int32 [32, 16], P(('narrow', 'wide')), may hold values from 8 to 32, as said below
- segment_ids: int32 [32768], P(('narrow', 'wide')), may hold values from 0 to 13, as said below
- positions: int32 [32768], P(('narrow', 'wide')), may hold values from 0 to 3135, as said below
- cotangent: bfloat16 [32768, 768], P(('narrow', 'wide')), may hold values from -6 to 6
- input_weight: bfloat16 [768, 2304], P('wide'), may hold values from -0.21875 to 0.21875
- output_weight: bfloat16 [768, 768], P('wide'), may hold values from -0.875 to 0.875
- up_weight: bfloat16 [768, 3072], P('wide'), may hold values from -0.21875 to 0.21875
- down_weight: bfloat16 [3072, 768], P('wide'), may hold values from -0.109375 to 0.109375
- pre_gain: bfloat16 [768], P('wide'), may hold values from 0.099609375 to 1.8984375
- pre_bias: bfloat16 [768], P('wide'), may hold values from -3 to 3
- query_bias: bfloat16 [768], P('wide'), may hold values from -3 to 3
- value_bias: bfloat16 [768], P('wide'), may hold values from -3 to 3
- output_bias: bfloat16 [768], P('wide'), may hold values from -3 to 3
- mid_gain: bfloat16 [768], P('wide'), may hold values from 0.099609375 to 1.8984375
- mid_bias: bfloat16 [768], P('wide'), may hold values from -3 to 3
- up_bias: bfloat16 [3072], P('wide'), may hold values from -3 to 3
- down_bias: bfloat16 [768], P('wide'), may hold values from -3 to 3
Outputs:
- block_out: bfloat16 [32768, 768], P(('narrow', 'wide'))
- input_grad: bfloat16 [32768, 768], P(('narrow', 'wide'))
- grad_input_weight: float32 [768, 2304], P('wide')
- grad_output_weight: float32 [768, 768], P('wide')
- grad_up_weight: float32 [768, 3072], P('wide')
- grad_down_weight: float32 [3072, 768], P('wide')
- grad_pre_gain: float32 [768], P('wide')
- grad_pre_bias: float32 [768], P('wide')
- grad_query_bias: float32 [768], P('wide')
- grad_value_bias: float32 [768], P('wide')
- grad_output_bias: float32 [768], P('wide')
- grad_mid_gain: float32 [768], P('wide')
- grad_mid_bias: float32 [768], P('wide')
- grad_up_bias: float32 [3072], P('wide')
- grad_down_bias: float32 [768], P('wide')
Inputs may be any that keep to these rules, and one draw needn't show every extreme that they name: `frame_counts`: each packed sequence fills its clip slots in order; a slot's clip has 8, 16 or 32 frames, short clips being the most common; slots that the sequence's rows never reach still hold a frame count. `segment_ids`: within a sequence the slot number never falls and starts at 0; a clip of 8, 16 or 32 frames holds 78, 157 or 314 rows times 1024 / 1024 (rounded down, at least 1), except that the sequence's end may cut its last clip. `positions`: index of a row's tubelet in its clip's grid of (frames / 2) x 14 x 14 tubelets, below that grid's size.
All inputs are finite; a program needn't handle non-finite values.
Results may differ from a plain program's by a relative error of at most 0.019.
Values may be sent and summed in bfloat16 or wider, within the bound.
No kernel may reach another device: no remote copies, remote signals or barrier semaphores. Data moves between devices by JAX's collectives and lax.ppermute only.
A program may use at most 192 MiB of HBM per device.

v0:
```python
from functools import partial
import math
import jax
import jax.numpy as jnp
from jax import lax
from jax.sharding import PartitionSpec as P

D = 768
HEADS = 12
HEAD_DIM = 64


def layer_norm(values, gain, shift):
    center = values - jnp.mean(values, axis=-1, keepdims=True)
    spread = jnp.mean(center * center, axis=-1, keepdims=True)
    return center * lax.rsqrt(spread + 1e-06) * gain + shift


def position_table(position_ids, frame_row):
    tubelet = position_ids // 196
    within = position_ids % 196
    first = tubelet.astype(jnp.float32) * 16.0 / frame_row.astype(jnp.float32)
    second = (within // 14).astype(jnp.float32)
    third = (within % 14).astype(jnp.float32)
    channel = jnp.arange(D, dtype=jnp.int32)
    picker = (channel % 3)[None, :]
    rate = jnp.exp(-(6.0 * (channel // 6).astype(jnp.float32) / D) * math.log(10000.0))
    coordinate = jnp.where(
        picker == 0, first[:, None], jnp.where(picker == 1, second[:, None], third[:, None])
    )
    angle = coordinate * rate[None, :]
    return jnp.where((channel // 3 % 2)[None, :] == 1, jnp.cos(angle), jnp.sin(angle))


def to_items(values, seq_count, length):
    pair_count = HEADS // 2
    shaped = values.reshape(seq_count, length, pair_count, 2, HEAD_DIM).transpose(0, 2, 1, 3, 4)
    return shaped.reshape(seq_count * pair_count, length, 2, HEAD_DIM)


def from_items(items, seq_count, length):
    pair_count = HEADS // 2
    shaped = items.reshape(seq_count, pair_count, length, 2, HEAD_DIM).transpose(0, 2, 1, 3, 4)
    return shaped.reshape(seq_count * length, D)


def masked_scores(queries, key_rows, labels):
    scores = jnp.einsum(
        "qhd,khd->hqk", queries, key_rows, preferred_element_type=jnp.float32
    ) * HEAD_DIM ** (-0.5)
    allowed = labels[:, None] == labels[None, :]
    return jnp.where(allowed[None], scores, -1e30)


def pair_forward(packed):
    queries, key_rows, values, labels = packed
    scores = masked_scores(queries, key_rows, labels)
    peak_score = jnp.max(scores, axis=-1, keepdims=True)
    expo_scores = jnp.exp(scores - peak_score)
    total_mass = jnp.sum(expo_scores, axis=-1, keepdims=True)
    probabilities = expo_scores / total_mass
    attended = jnp.einsum(
        "hqk,khd->qhd",
        probabilities.astype(jnp.bfloat16),
        values,
        preferred_element_type=jnp.float32,
    )
    return (attended, (peak_score + jnp.log(total_mass))[..., 0])


def pair_backward(packed):
    queries, key_rows, values, labels, grad_out, log_mass = packed
    scores = masked_scores(queries, key_rows, labels)
    probabilities = jnp.exp(scores - log_mass[..., None])
    grad_probs = jnp.einsum("qhd,khd->hqk", grad_out, values, preferred_element_type=jnp.float32)
    weighted = jnp.sum(probabilities * grad_probs, axis=-1, keepdims=True)
    grad_scores = (probabilities * (grad_probs - weighted)).astype(jnp.bfloat16)
    scale = HEAD_DIM ** (-0.5)
    grad_query = (
        jnp.einsum("hqk,khd->qhd", grad_scores, key_rows, preferred_element_type=jnp.float32)
        * scale
    )
    grad_keys = (
        jnp.einsum("hqk,qhd->khd", grad_scores, queries, preferred_element_type=jnp.float32) * scale
    )
    grad_values = jnp.einsum(
        "hqk,qhd->khd",
        probabilities.astype(jnp.bfloat16),
        grad_out,
        preferred_element_type=jnp.float32,
    )
    return (grad_query, grad_keys, grad_values)


def reduce_feedforward(gradients):
    shares = (
        lax.psum_scatter(
            gradients[0].astype(jnp.bfloat16), "wide", scatter_dimension=0, tiled=True
        ).astype(jnp.float32),
        lax.psum_scatter(
            gradients[1].astype(jnp.bfloat16), "wide", scatter_dimension=0, tiled=True
        ).astype(jnp.float32),
        lax.psum_scatter(
            gradients[2].astype(jnp.bfloat16), "wide", scatter_dimension=0, tiled=True
        ).astype(jnp.float32),
        lax.psum_scatter(
            gradients[3].astype(jnp.bfloat16), "wide", scatter_dimension=0, tiled=True
        ).astype(jnp.float32),
        lax.psum_scatter(
            gradients[4].astype(jnp.bfloat16), "wide", scatter_dimension=0, tiled=True
        ).astype(jnp.float32),
        lax.psum_scatter(
            gradients[5].astype(jnp.bfloat16), "wide", scatter_dimension=0, tiled=True
        ).astype(jnp.float32),
    )
    return (
        lax.psum(shares[0].astype(jnp.bfloat16), "narrow").astype(jnp.float32),
        lax.psum(shares[1].astype(jnp.bfloat16), "narrow").astype(jnp.float32),
        lax.psum(shares[2].astype(jnp.bfloat16), "narrow").astype(jnp.float32),
        lax.psum(shares[3].astype(jnp.bfloat16), "narrow").astype(jnp.float32),
        lax.psum(shares[4].astype(jnp.bfloat16), "narrow").astype(jnp.float32),
        lax.psum(shares[5].astype(jnp.bfloat16), "narrow").astype(jnp.float32),
    )


def reduce_attention(gradients):
    shares = (
        lax.psum_scatter(
            gradients[0].astype(jnp.bfloat16), "wide", scatter_dimension=0, tiled=True
        ).astype(jnp.float32),
        lax.psum_scatter(
            gradients[1].astype(jnp.bfloat16), "wide", scatter_dimension=0, tiled=True
        ).astype(jnp.float32),
        lax.psum_scatter(
            gradients[2].astype(jnp.bfloat16), "wide", scatter_dimension=0, tiled=True
        ).astype(jnp.float32),
        lax.psum_scatter(
            gradients[3].astype(jnp.bfloat16), "wide", scatter_dimension=0, tiled=True
        ).astype(jnp.float32),
        lax.psum_scatter(
            gradients[4].astype(jnp.bfloat16), "wide", scatter_dimension=0, tiled=True
        ).astype(jnp.float32),
        lax.psum_scatter(
            gradients[5].astype(jnp.bfloat16), "wide", scatter_dimension=0, tiled=True
        ).astype(jnp.float32),
        lax.psum_scatter(
            gradients[6].astype(jnp.bfloat16), "wide", scatter_dimension=0, tiled=True
        ).astype(jnp.float32),
    )
    return (
        lax.psum(shares[0].astype(jnp.bfloat16), "narrow").astype(jnp.float32),
        lax.psum(shares[1].astype(jnp.bfloat16), "narrow").astype(jnp.float32),
        lax.psum(shares[2].astype(jnp.bfloat16), "narrow").astype(jnp.float32),
        lax.psum(shares[3].astype(jnp.bfloat16), "narrow").astype(jnp.float32),
        lax.psum(shares[4].astype(jnp.bfloat16), "narrow").astype(jnp.float32),
        lax.psum(shares[5].astype(jnp.bfloat16), "narrow").astype(jnp.float32),
        lax.psum(shares[6].astype(jnp.bfloat16), "narrow").astype(jnp.float32),
    )


def per_device(
    tokens,
    frame_counts,
    segment_ids,
    positions,
    cotangent,
    input_weight,
    output_weight,
    up_weight,
    down_weight,
    pre_gain,
    pre_bias,
    query_bias,
    value_bias,
    output_bias,
    mid_gain,
    mid_bias,
    up_bias,
    down_bias,
):
    seq_count = frame_counts.shape[0]
    row_total = tokens.shape[0]
    length = row_total // seq_count
    pair_count = HEADS // 2
    labels = segment_ids.reshape(seq_count, length)
    clip_index = jnp.arange(frame_counts.shape[1], dtype=jnp.int32)
    matches = labels[:, :, None] == clip_index[None, None, :]
    frame_row = jnp.sum(jnp.where(matches, frame_counts[:, None, :], 0), axis=2).reshape(row_total)
    start = tokens.astype(jnp.float32) + position_table(positions, frame_row)
    (
        full_input,
        full_output,
        full_pre_gain,
        full_pre_bias,
        full_query_bias,
        full_value_bias,
        full_output_bias,
    ) = (
        lax.all_gather(input_weight, "wide", axis=0, tiled=True),
        lax.all_gather(output_weight, "wide", axis=0, tiled=True),
        lax.all_gather(pre_gain, "wide", axis=0, tiled=True),
        lax.all_gather(pre_bias, "wide", axis=0, tiled=True),
        lax.all_gather(query_bias, "wide", axis=0, tiled=True),
        lax.all_gather(value_bias, "wide", axis=0, tiled=True),
        lax.all_gather(output_bias, "wide", axis=0, tiled=True),
    )
    pre_gain_f = full_pre_gain.astype(jnp.float32)
    normed_low = layer_norm(start, pre_gain_f, full_pre_bias.astype(jnp.float32)).astype(
        jnp.bfloat16
    )
    query_bias_f = full_query_bias.astype(jnp.float32)
    joint_bias = jnp.concatenate(
        [query_bias_f, jnp.zeros_like(query_bias_f), full_value_bias.astype(jnp.float32)]
    )
    mixed_low = (
        jnp.dot(normed_low, full_input, preferred_element_type=jnp.float32) + joint_bias
    ).astype(jnp.bfloat16)
    item_labels = jnp.broadcast_to(labels[:, None, :], (seq_count, pair_count, length)).reshape(
        seq_count * pair_count, length
    )
    query_items = to_items(mixed_low[:, :D], seq_count, length)
    key_items = to_items(mixed_low[:, D : 2 * D], seq_count, length)
    value_items = to_items(mixed_low[:, 2 * D :], seq_count, length)
    attended_items, log_mass = lax.map(
        pair_forward, (query_items, key_items, value_items, item_labels)
    )
    attended_low = from_items(attended_items, seq_count, length).astype(jnp.bfloat16)
    middle = (
        start
        + jnp.dot(attended_low, full_output, preferred_element_type=jnp.float32)
        + full_output_bias.astype(jnp.float32)
    )
    full_up, full_down, full_mid_gain, full_mid_bias, full_up_bias, full_down_bias = (
        lax.all_gather(up_weight, "wide", axis=0, tiled=True),
        lax.all_gather(down_weight, "wide", axis=0, tiled=True),
        lax.all_gather(mid_gain, "wide", axis=0, tiled=True),
        lax.all_gather(mid_bias, "wide", axis=0, tiled=True),
        lax.all_gather(up_bias, "wide", axis=0, tiled=True),
        lax.all_gather(down_bias, "wide", axis=0, tiled=True),
    )
    normed_two = layer_norm(
        middle, full_mid_gain.astype(jnp.float32), full_mid_bias.astype(jnp.float32)
    )
    normed_two_low = normed_two.astype(jnp.bfloat16)
    upward = jnp.dot(
        normed_two_low, full_up, preferred_element_type=jnp.float32
    ) + full_up_bias.astype(jnp.float32)
    gelu_exact = partial(jax.nn.gelu, approximate=False)
    active_low = gelu_exact(upward).astype(jnp.bfloat16)
    block_out = (
        middle
        + jnp.dot(active_low, full_down, preferred_element_type=jnp.float32)
        + full_down_bias.astype(jnp.float32)
    ).astype(jnp.bfloat16)
    up_back, down_back, mid_gain_back = (
        lax.all_gather(up_weight, "wide", axis=0, tiled=True),
        lax.all_gather(down_weight, "wide", axis=0, tiled=True),
        lax.all_gather(mid_gain, "wide", axis=0, tiled=True),
    )
    grad_top = cotangent.astype(jnp.float32)
    grad_down_bias = jnp.sum(grad_top, axis=0)
    grad_down_weight = jnp.einsum(
        "rf,rd->fd", active_low, cotangent, preferred_element_type=jnp.float32
    )
    grad_active = jnp.einsum("rd,fd->rf", cotangent, down_back, preferred_element_type=jnp.float32)
    _, gelu_pull = jax.vjp(gelu_exact, upward)
    grad_upward_low = gelu_pull(grad_active)[0].astype(jnp.bfloat16)
    grad_up_bias = jnp.sum(grad_upward_low.astype(jnp.float32), axis=0)
    grad_up_weight = jnp.einsum(
        "rd,rf->df", normed_two_low, grad_upward_low, preferred_element_type=jnp.float32
    )
    grad_normed_two = jnp.einsum(
        "rf,df->rd", grad_upward_low, up_back, preferred_element_type=jnp.float32
    )
    mid_gain_f = mid_gain_back.astype(jnp.float32)
    _, norm_pull = jax.vjp(layer_norm, middle, mid_gain_f, jnp.zeros_like(mid_gain_f))
    grad_middle_part, grad_mid_gain, grad_mid_bias = norm_pull(grad_normed_two)
    grad_middle = grad_top + grad_middle_part
    out_up_weight, out_down_weight, out_mid_gain, out_mid_bias, out_up_bias, out_down_bias = (
        reduce_feedforward(
            (
                grad_up_weight,
                grad_down_weight,
                grad_mid_gain,
                grad_mid_bias,
                grad_up_bias,
                grad_down_bias,
            )
        )
    )
    input_back, output_back, pre_gain_back = (
        lax.all_gather(input_weight, "wide", axis=0, tiled=True),
        lax.all_gather(output_weight, "wide", axis=0, tiled=True),
        lax.all_gather(pre_gain, "wide", axis=0, tiled=True),
    )
    grad_branch_low = grad_middle.astype(jnp.bfloat16)
    grad_output_bias = jnp.sum(grad_branch_low.astype(jnp.float32), axis=0)
    grad_output_weight = jnp.einsum(
        "rd,re->de", attended_low, grad_branch_low, preferred_element_type=jnp.float32
    )
    grad_attended_low = jnp.einsum(
        "re,de->rd", grad_branch_low, output_back, preferred_element_type=jnp.float32
    ).astype(jnp.bfloat16)
    grad_items = to_items(grad_attended_low, seq_count, length)
    grad_query, grad_keys, grad_values = lax.map(
        pair_backward, (query_items, key_items, value_items, item_labels, grad_items, log_mass)
    )
    grad_mixed_low = jnp.concatenate(
        [
            from_items(grad_query, seq_count, length),
            from_items(grad_keys, seq_count, length),
            from_items(grad_values, seq_count, length),
        ],
        axis=1,
    ).astype(jnp.bfloat16)
    grad_query_bias = jnp.sum(grad_mixed_low[:, :D].astype(jnp.float32), axis=0)
    grad_value_bias = jnp.sum(grad_mixed_low[:, 2 * D :].astype(jnp.float32), axis=0)
    grad_input_weight = jnp.einsum(
        "rd,re->de", normed_low, grad_mixed_low, preferred_element_type=jnp.float32
    )
    grad_normed = jnp.einsum(
        "re,de->rd", grad_mixed_low, input_back, preferred_element_type=jnp.float32
    )
    pre_gain_b = pre_gain_back.astype(jnp.float32)
    _, first_pull = jax.vjp(layer_norm, start, pre_gain_b, jnp.zeros_like(pre_gain_b))
    grad_start_part, grad_pre_gain, grad_pre_bias = first_pull(grad_normed)
    input_grad = (grad_middle + grad_start_part).astype(jnp.bfloat16)
    (
        out_input_weight,
        out_output_weight,
        out_pre_gain,
        out_pre_bias,
        out_query_bias,
        out_value_bias,
        out_output_bias,
    ) = reduce_attention(
        (
            grad_input_weight,
            grad_output_weight,
            grad_pre_gain,
            grad_pre_bias,
            grad_query_bias,
            grad_value_bias,
            grad_output_bias,
        )
    )
    return (
        block_out,
        input_grad,
        out_input_weight,
        out_output_weight,
        out_up_weight,
        out_down_weight,
        out_pre_gain,
        out_pre_bias,
        out_query_bias,
        out_value_bias,
        out_output_bias,
        out_mid_gain,
        out_mid_bias,
        out_up_bias,
        out_down_bias,
    )


def solution(mesh):
    in_specs = (
        P(("narrow", "wide"), None),
        P(("narrow", "wide"), None),
        P(("narrow", "wide")),
        P(("narrow", "wide")),
        P(("narrow", "wide"), None),
        P("wide", None),
        P("wide", None),
        P("wide", None),
        P("wide", None),
        P("wide"),
        P("wide"),
        P("wide"),
        P("wide"),
        P("wide"),
        P("wide"),
        P("wide"),
        P("wide"),
        P("wide"),
    )
    out_specs = (
        P(("narrow", "wide"), None),
        P(("narrow", "wide"), None),
        P("wide", None),
        P("wide", None),
        P("wide", None),
        P("wide", None),
        P("wide"),
        P("wide"),
        P("wide"),
        P("wide"),
        P("wide"),
        P("wide"),
        P("wide"),
        P("wide"),
        P("wide"),
    )
    return jax.shard_map(
        per_device, mesh=mesh, in_specs=in_specs, out_specs=out_specs, check_vma=False
    )
```

profile of v0, /device:TPU:0, one launch (start us, length us, event | category | flops | bytes accessed | tf_op | source)
XLA Modules:
  0.0 671.5 jit_solution(14226232161853406409)
XLA Ops:
  12.9 13.1 %fusion.92 = f32[1024]{0:T(1024)S(1)} fusion(f32[768]{0:T(1024)S(1)} %fusion.71, f32[1024]{0:T(1024)S(1)} %get-tuple-element.254, f32[1024]{0:T(1024)S(1)} %get-tuple-element.253, pred[768]{0:T(1024)(128)(4,1)S(1)} %get-tuple-element.267, f32[1024]{0:T(1024)S(1)} %fusion.76, pred[768]{0:T(1024)(128)(4,1)S(1)} %fusion.81, ...), kind=kLoop, calls=%fused_computation.165 | loop fusion | flops 5504000 | bytes 1594624 | tf_op jit(solution)/shard_map/reduce_sum | solution.py:14
  26.0 13.3 %multiply_reduce_fusion.6 = f32[1024]{0:T(1024)S(1)} fusion(f32[1024]{0:T(1024)S(1)} %broadcast_multiply_fusion.1, f32[768]{0:T(1024)S(1)} %fusion.71, f32[1024]{0:T(1024)S(1)} %get-tuple-element.254, f32[1024]{0:T(1024)S(1)} %get-tuple-element.253, pred[768]{0:T(1024)(128)(4,1)S(1)} %get-tuple-element.267, f32[1024]{0:T(1024)S(1)} %fusion.76, ...), kind=kLoop, calls=%fused_computation.97 | loop fusion | flops 7076864 | bytes 1598720 | tf_op jit(solution)/shard_map/reduce_sum | solution.py:15
  42.3 30.8 %all-reduce.18 = (bf16[768]{0:T(1024)(128)(2,1)S(1)}, bf16[768]{0:T(1024)(128)(2,1)S(1)}, bf16[768]{0:T(1024)(128)(2,1)S(1)}, bf16[768]{0:T(1024)(128)(2,1)S(1)}...) all-reduce(bf16[768]{0:T(1024)(128)(2,1)S(1)} %dynamic-update-slice, ...), channel_id=1, replica_groups=mesh['narrow'=4,'wide'=8] {'wide'}, use_global_device_ids=true, to_apply=%add.3 | all-reduce | flops 5376 | bytes 21504
  73.2 12.8 %all-gather = bf16[8,1,384]{2,1,0:T(2,128)(2,1)S(1)} all-gather(bf16[1,1,384]{2,1,0:T(2,128)(2,1)S(1)} %reshape.408), channel_id=1, replica_groups=mesh['narrow'=4,'wide'=8] {'wide'}, dimensions={0}, use_global_device_ids=true | all-gather | bytes 6912 | tf_op jit(solution)/shard_map/all_gather | solution.py:238
  87.7 14.2 %add_convert_fusion.13 = bf16[1024,768]{0,1:T(8,128)(2,1)} fusion(f32[768]{0:T(1024)S(1)} %convert_element_type.208, f32[768]{0:T(1024)S(1)} %convert_element_type.207, f32[1024]{0:T(1024)S(1)} %fusion.86, f32[1024]{0:T(1024)S(1)} %broadcast_multiply_fusion.1, f32[768]{0:T(1024)S(1)} %fusion.71, f32[1024]{0:T(1024)S(1)} %get-tuple-element.254, ...), kind=kLoop, calls=%fused_computation.96.clone.clone.2 | loop fusion | flops 8650752 | bytes 3177728 | tf_op jit(solution)/shard_map/rd,re->de/dot_general | solution.py:318
  102.0 18.0 %add_convert_fusion.1 = bf16[1024,2304]{1,0:T(8,128)(2,1)S(1)} fusion(bf16[768,2304]{1,0:T(8,128)(2,1)} %all-gather.6.cloned.1.call-done, f32[2304]{0:T(1024)S(1)} %pad_maximum_fusion.3, f32[768]{0:T(1024)S(1)} %convert_element_type.208, f32[768]{0:T(1024)S(1)} %convert_element_type.207, f32[1024]{0:T(1024)S(1)} %fusion.86, ...), kind=kOutput, calls=%fused_computation.79 | convolution fusion | flops 3637248000 | bytes 9871616 | tf_op jit(solution)/shard_map/dot_general | solution.py:216
  129.3 63.2 %while.26 = (s32[]{:T(128)}, bf16[6,1024,2,64]{1,3,2,0:T(8,128)(2,1)}, f32[6,2,1024]{2,1,0:T(2,128)}, bf16[6,1024,2,64]{1,3,2,0:T(8,128)(2,1)}, s32[6,1024]{1,0:...) while((s32[]{:T(128)}, ...), condition=%wide.region_6.7_spmd, body=%wide.region_3.6_spmd.sunk | while | flops 563083264 | bytes 30751320 | solution.py:224
  135.4 4.4 fusion.143
  145.9 4.4 fusion.143
  156.5 4.4 fusion.143
  167.0 4.4 fusion.143
  177.5 4.4 fusion.143
  188.1 4.4 fusion.143
  192.5 15.3 %fusion.99 = (f32[1024]{0:T(1024)S(1)}, f32[1024,768]{0,1:T(8,128)S(1)}) fusion(f32[768]{0:T(1024)S(1)} %convert_element_type.217, bf16[1024,768]{0,1:T(8,128)(2,1)} %bitcast.32, bf16[768,768]{1,0:T(8,128)(2,1)} %all-gather.8.cloned.1.call-done, f32[768]{0:T(1024)S(1)} %fusion.71, f32[1024]{0:T(1024)S(1)} %get-tuple-element.254, ...), kind=kOutput, calls=%fused_computation.170 | convolution fusion | flops 1215036416 | bytes 7495936 | tf_op jit(solution)/shard_map/dot_general | solution.py:230
  210.0 38.1 %multiply_convert_fusion.1 = (bf16[1024,3072]{1,0:T(8,128)(2,1)}, f32[1024,3072]{1,0:T(8,128)}, f32[1024,3072]{1,0:T(8,128)}) fusion(f32[3072]{0:T(1024)S(1)} %bitcast.182, bf16[768,3072]{1,0:T(8,128)(2,1)} %all-gather.10.cloned.1.call-done, f32[1024,768]{0,1:T(8,128)} %copy-done.2, f32[768]{0:T(1024)S(1)} %convert_element_type.219, ...), kind=kOutput, calls=%fused_computation.65 | convolution fusion | flops 5043388416 | bytes 39348224 | tf_op jit(solution)/shard_map/dot_general | solution.py:245
  248.0 17.4 %fusion.102 = (bf16[3072]{0:T(1024)(128)(2,1)}, bf16[1024,3072]{1,0:T(8,128)(2,1)}) fusion(f32[1024,3072]{1,0:T(8,128)} %get-tuple-element.245, bf16[1024,768]{1,0:T(8,128)(2,1)S(1)} %copy-done.10, bf16[3072,768]{1,0:T(8,128)(2,1)} %all-gather.12.cloned.1.call-done, f32[1024,3072]{1,0:T(8,128)} %get-tuple-element.259, f32[3072]{0:T(1024)S(1)} %bitcast.183), kind=kOutput, calls=%fused_computation.173 | convolution fusion | flops 4882166784 | bytes 37767168 | tf_op jit(solution)/shard_map/rd,fd->rf/dot_general | solution.py:265
  265.4 10.7 %fusion.101 = (bf16[768]{0:T(1024)(128)(2,1)}, f32[1024,768]{1,0:T(8,128)}) fusion(bf16[1024,3072]{1,0:T(8,128)(2,1)} %get-tuple-element.265, bf16[768,3072]{1,0:T(8,128)(2,1)} %all-gather.10.cloned.1.call-done), kind=kOutput, calls=%fused_computation.172 | convolution fusion | flops 4832623616 | bytes 14157312 | tf_op jit(solution)/shard_map/rf,df->rd/dot_general | solution.py:272
  276.2 3.7 copy.91
  279.8 3.5 multiply_reduce_fusion.1
  287.0 3.8 convolution_convert_fusion.4
  291.0 4.3 convolution_convert_fusion.3
  299.4 130.1 %while.27 = (s32[]{:T(128)}, bf16[6,1024,2,64]{1,3,2,0:T(8,128)(2,1)}, bf16[6,1024,2,64]{1,3,2,0:T(8,128)(2,1)}, bf16[6,1024,2,64]{1,3,2,0:T(8,128)(2,1)}, bf16[...) while((s32[]{:T(128)}, ...), condition=%wide.region_13.14_spmd, body=%wide.region_11.13_spmd.sunk | while | flops 1374943232 | bytes 83174576 | solution.py:305
  304.0 4.2 multiply_reduce_fusion.8
  317.0 4.2 fusion.155
  325.7 4.2 multiply_reduce_fusion.8
  338.7 4.2 fusion.155
  347.3 4.2 multiply_reduce_fusion.8
  360.4 4.2 fusion.155
  369.0 4.2 multiply_reduce_fusion.8
  382.0 4.2 fusion.155
  390.6 4.2 multiply_reduce_fusion.8
  397.5 3.2 fusion.154
  403.7 4.2 fusion.155
  412.3 4.2 multiply_reduce_fusion.8
  419.2 3.2 fusion.154
  425.3 4.2 fusion.155
  429.5 8.5 %convolution_convert_fusion.2 = bf16[768,2304]{1,0:T(8,128)(2,1)} fusion(bf16[1024,768]{0,1:T(8,128)(2,1)} %bitcast.51, bf16[1024,768]{0,1:T(8,128)(2,1)} %bitcast.177, bf16[1024,768]{0,1:T(8,128)(2,1)} %bitcast.174, bf16[1024,768]{0,1:T(8,128)(2,1)} %add_convert_fusion.13), kind=kOutput, calls=%fused_computation.82 | convolution fusion | flops 3639803904 | bytes 9830400 | tf_op jit(solution)/shard_map/rd,re->de/dot_general | solution.py:318
  438.6 10.0 %convolution_convert_fusion.1 = bf16[768,3072]{1,0:T(8,128)(2,1)} fusion(bf16[1024,3072]{1,0:T(8,128)(2,1)} %get-tuple-element.265, f32[1024,768]{0,1:T(8,128)S(1)} %copy-done.3, f32[768]{0:T(1024)S(1)} %copy-done.49, f32[768]{0:T(1024)S(1)} %convert_element_type.218, f32[1024]{0:T(1024)S(1)} %fusion.87, f32[1024]{0:T(1024)S(1)} %broadcast_multiply_fusion), kind=kOutput, calls=%fused_computation.81 | convolution fusion | flops 4838129664 | bytes 14170112 | tf_op jit(solution)/shard_map/rd,rf->df/dot_general | solution.py:269
  450.0 9.8 %convolution_convert_fusion = bf16[3072,768]{1,0:T(8,128)(2,1)} fusion(bf16[1024,3072]{1,0:T(8,128)(2,1)} %get-tuple-element.244, bf16[1024,768]{1,0:T(8,128)(2,1)S(1)} %copy-done.11), kind=kOutput, calls=%fused_computation.80 | convolution fusion | flops 4834197504 | bytes 12582912 | tf_op jit(solution)/shard_map/rf,rd->fd/dot_general | solution.py:262
  461.9 8.7 %fusion.100 = (bf16[768]{0:T(1024)(128)(2,1)S(1)}, f32[1024,768]{1,0:T(8,128)}) fusion(bf16[768,2304]{1,0:T(8,128)(2,1)} %all-gather.6.cloned.1.call-done, bf16[1024,768]{0,1:T(8,128)(2,1)} %bitcast.51, bf16[1024,768]{0,1:T(8,128)(2,1)} %bitcast.178, bf16[1024,768]{0,1:T(8,128)(2,1)S(1)} %bitcast.175), kind=kOutput, calls=%fused_computation.171 | convolution fusion | flops 3638820096 | bytes 11404800 | tf_op jit(solution)/shard_map/re,de->rd/dot_general | solution.py:321
  476.7 14.3 %multiply_reduce_fusion.3 = f32[1024]{0:T(1024)S(1)} fusion(f32[1024,768]{0,1:T(8,128)S(1)} %copy.92, f32[768]{0:T(1024)S(1)} %copy-done.30, f32[1024]{0:T(1024)S(1)} %copy-done.28, f32[768]{0:T(1024)S(1)} %copy-done.20, f32[1024]{0:T(1024)S(1)} %copy-done.24, f32[1024]{0:T(1024)S(1)} %copy-done.22, pred[768]{0:T(1024)(128)(4,1)S(1)} %copy-done.38, ...), kind=kLoop, calls=%fused_computation.89 | loop fusion | flops 7863296 | bytes 4747520 | tf_op jit(solution)/shard_map/transpose(jvp())/reduce_sum | solution.py:16
  491.1 13.4 %multiply_reduce_fusion.2 = (bf16[768]{0:T(1024)(128)(2,1)S(1)}, f32[1024]{0:T(1024)S(1)}) fusion(f32[1024,768]{0,1:T(8,128)S(1)} %copy.92, f32[1024]{0:T(1024)S(1)} %copy-done.32, f32[1024]{0:T(1024)S(1)} %copy-done.28, f32[768]{0:T(1024)S(1)} %copy-done.20, f32[1024]{0:T(1024)S(1)} %copy-done.24, f32[1024]{0:T(1024)S(1)} %copy-done.22, ...), kind=kLoop, calls=%fused_computation.87 | loop fusion | flops 12581120 | bytes 4757248 | tf_op jit(solution)/shard_map/transpose(jvp())/reduce_sum | solution.py:16
  504.6 27.9 %all-reduce.17 = (bf16[768]{0:T(1024)(128)(2,1)S(1)}, bf16[768]{0:T(1024)(128)(2,1)S(1)}, bf16[768]{0:T(1024)(128)(2,1)S(1)}, bf16[768]{0:T(1024)(128)(2,1)S(1)}...) all-reduce(bf16[768]{0:T(1024)(128)(2,1)S(1)} %dynamic-update-slice, ...), channel_id=1, replica_groups=mesh['narrow'=4,'wide'=8] {'wide'}, use_global_device_ids=true, to_apply=%add.7 | all-reduce | flops 9984 | bytes 39936
  533.1 10.2 %all-reduce.19 = (bf16[96]{0:T(256)(128)(2,1)S(1)}, bf16[96]{0:T(256)(128)(2,1)S(1)}, bf16[96]{0:T(256)(128)(2,1)S(1)}, bf16[96]{0:T(256)(128)(2,1)S(1)}, bf16[9...) all-reduce(bf16[96]{0:T(256)(128)(2,1)S(1)} %dynamic-slice.9, ...), channel_id=1, replica_groups=mesh['narrow'=4,'wide'=8] {'narrow'}, use_global_device_ids=true, to_apply=%region_26.27 | all-reduce | flops 1152 | bytes 4608 | tf_op jit(solution)/shard_map/psum | solution.py:153
  548.0 16.3 %add_convert_fusion.2 = bf16[1024,768]{0,1:T(8,128)(2,1)} fusion(f32[1024,768]{0,1:T(8,128)} %copy-done.6, bf16[1024,768]{0,1:T(8,128)(2,1)} %copy.90, f32[1024]{0:T(1024)S(1)} %negate_multiply_fusion.1, f32[1024]{0:T(1024)S(1)} %copy-done.34, f32[1024]{0:T(1024)S(1)} %multiply_multiply_fusion.5, f32[1024]{0:T(1024)S(1)} %copy-done.28, ...), kind=kLoop, calls=%fused_computation.88 | loop fusion | flops 14155776 | bytes 11051264 | tf_op jit(solution)/shard_map/convert_element_type | solution.py:327
  567.1 25.3 %reduce-scatter.11.cloned.1.call-done = bf16[384,768]{1,0:T(8,128)(2,1)} async-done(((bf16[3072,768]{1,0:T(8,128)(2,1)}), bf16[384,768]{1,0:T(8,128)(2,1)}) %reduce-scatter.11.cloned.1.call-update) | async-done | bytes 589840 | tf_op jit(solution)/shard_map/reduce_scatter | solution.py:100
  592.4 9.5 %add_convert_fusion.3 = bf16[1024,768]{0,1:T(8,128)(2,1)} fusion(f32[1024,768]{0,1:T(8,128)S(1)} %copy-done.4, bf16[1024,3072]{1,0:T(8,128)(2,1)} %get-tuple-element.244, bf16[3072,768]{1,0:T(8,128)(2,1)} %all-gather.12.cloned.1.call-done, f32[768]{0:T(1024)S(1)} %convert_element_type.223), kind=kOutput, calls=%fused_computation.92 | convolution fusion | flops 4834197504 | bytes 15731712 | tf_op jit(solution)/shard_map/dot_general | solution.py:252
  604.5 54.0 %all-reduce.23.cloned.1.call-done = (bf16[96,2304]{1,0:T(8,128)(2,1)}, bf16[96,768]{1,0:T(8,128)(2,1)}, bf16[96,3072]{1,0:T(8,128)(2,1)}, bf16[384,768]{1,0:T(8,128)(2,1)}) async-done(((bf16[96,2304]{1,0:T(8,128)(2,1)}, bf16[96,768]{1,0:T(8,128)(2,1)}, bf16[96,3072]{1,0:T(8,128)(2,1)}, bf16[384,768]{1,0:T(8,128)(2,1)}), (bf16[96,2304]{1,0:T(8,128)(2,1)}, bf16[96,768]{1,0:T(8,128)(2,1)}, ...) | async-done | bytes 1769488 | tf_op jit(solution)/shard_map/psum | solution.py:151
  (327 shorter events, 164.1 us)
Async XLA Ops:
  7.2 5.7 copy-start.39
  7.2 5.6 copy-start.53
  7.2 5.6 copy-start.40
  7.2 94.7 %all-gather.6.cloned.1.call-start = ((), (), s32[]{:S(2)}) async-start(), calls=%async_computation.4 | async-start | bytes 3981312 | tf_op jit(solution)/shard_map/all_gather | solution.py:199
  7.9 184.5 %all-gather.8.cloned.1.call-start = ((), (), s32[]{:S(2)}) async-start(), calls=%async_computation.5 | async-start | bytes 1327104 | tf_op jit(solution)/shard_map/all_gather | solution.py:200
  8.7 201.2 %all-gather.10.cloned.1.call-start = ((), (), s32[]{:S(2)}) async-start(), calls=%async_computation.6 | async-start | bytes 5308416 | tf_op jit(solution)/shard_map/all_gather | solution.py:234
  9.4 238.6 %all-gather.12.cloned.1.call-start = ((), (), s32[]{:S(2)}) async-start(), calls=%async_computation.7 | async-start | bytes 5308416 | tf_op jit(solution)/shard_map/all_gather | solution.py:235
  10.0 557.1 %reduce-scatter.7.cloned.1.call-start = ((), (), s32[]{:S(2)}) async-start(), calls=%async_computation.9 | async-start | bytes 1327104 | tf_op jit(solution)/shard_map/reduce_scatter | solution.py:131
  10.1 182.4 %copy-start.35 = (pred[768]{0:T(1024)(128)(4,1)}, pred[768]{0:T(1024)(128)(4,1)S(1)}, u32[]{:S(2)}) copy-start(pred[768]{0:T(1024)(128)(4,1)S(1)} %get-tuple-element.266) | copy-start | bytes 2308
  10.1 182.4 %copy-start.37 = (pred[768]{0:T(1024)(128)(4,1)}, pred[768]{0:T(1024)(128)(4,1)S(1)}, u32[]{:S(2)}) copy-start(pred[768]{0:T(1024)(128)(4,1)S(1)} %get-tuple-element.267) | copy-start | bytes 2308
  10.1 182.4 %copy-start.19 = (f32[768]{0:T(1024)}, f32[768]{0:T(1024)S(1)}, u32[]{:S(2)}) copy-start(f32[768]{0:T(1024)S(1)} %fusion.71) | copy-start | bytes 9220
  10.1 182.3 %copy-start.43 = (pred[768]{0:T(1024)(128)(4,1)}, pred[768]{0:T(1024)(128)(4,1)S(1)}, u32[]{:S(2)}) copy-start(pred[768]{0:T(1024)(128)(4,1)S(1)} %fusion.81) | copy-start | bytes 2308
  10.9 181.6 %copy-start.21 = (f32[1024]{0:T(1024)}, f32[1024]{0:T(1024)S(1)}, u32[]{:S(2)}) copy-start(f32[1024]{0:T(1024)S(1)} %get-tuple-element.253) | copy-start | bytes 12292
  10.9 181.6 %copy-start.23 = (f32[1024]{0:T(1024)}, f32[1024]{0:T(1024)S(1)}, u32[]{:S(2)}) copy-start(f32[1024]{0:T(1024)S(1)} %get-tuple-element.254) | copy-start | bytes 12292
  12.6 179.9 %copy-start = (bf16[1024,768]{0,1:T(8,128)(2,1)}, bf16[1024,768]{0,1:T(8,128)(2,1)S(1)}, u32[]{:S(2)}) copy-start(bf16[1024,768]{0,1:T(8,128)(2,1)S(1)} %copy.85) | copy-start | bytes 4718596
  12.6 26.7 %copy-start.51 = (u32[32]{0:T(128)S(1)}, u32[32]{0:T(128)}, u32[]{:S(2)}) copy-start(u32[32]{0:T(128)} %constant.211) | copy-start | bytes 388
  12.7 28.0 %copy-start.54 = (bf16[96]{0:T(256)(128)(2,1)S(1)}, bf16[96]{0:T(256)(128)(2,1)}, u32[]{:S(2)}) copy-start(bf16[96]{0:T(256)(128)(2,1)} %param.31) | copy-start | bytes 580
  12.7 28.2 %copy-start.55 = (bf16[96]{0:T(256)(128)(2,1)S(1)}, bf16[96]{0:T(256)(128)(2,1)}, u32[]{:S(2)}) copy-start(bf16[96]{0:T(256)(128)(2,1)} %param.32) | copy-start | bytes 580
  12.7 28.4 %copy-start.56 = (bf16[96]{0:T(256)(128)(2,1)S(1)}, bf16[96]{0:T(256)(128)(2,1)}, u32[]{:S(2)}) copy-start(bf16[96]{0:T(256)(128)(2,1)} %param.33) | copy-start | bytes 580
  12.7 28.6 %copy-start.57 = (bf16[96]{0:T(256)(128)(2,1)S(1)}, bf16[96]{0:T(256)(128)(2,1)}, u32[]{:S(2)}) copy-start(bf16[96]{0:T(256)(128)(2,1)} %param.34) | copy-start | bytes 580
  12.7 28.9 %copy-start.58 = (bf16[96]{0:T(256)(128)(2,1)S(1)}, bf16[96]{0:T(256)(128)(2,1)}, u32[]{:S(2)}) copy-start(bf16[96]{0:T(256)(128)(2,1)} %param.35) | copy-start | bytes 580
  12.7 29.1 %copy-start.59 = (bf16[96]{0:T(256)(128)(2,1)S(1)}, bf16[96]{0:T(256)(128)(2,1)}, u32[]{:S(2)}) copy-start(bf16[96]{0:T(256)(128)(2,1)} %param.36) | copy-start | bytes 580
  12.7 29.3 %copy-start.60 = (bf16[96]{0:T(256)(128)(2,1)S(1)}, bf16[96]{0:T(256)(128)(2,1)}, u32[]{:S(2)}) copy-start(bf16[96]{0:T(256)(128)(2,1)} %param.37) | copy-start | bytes 580
  12.7 60.4 %copy-start.52 = (bf16[384]{0:T(512)(128)(2,1)S(1)}, bf16[384]{0:T(512)(128)(2,1)}, u32[]{:S(2)}) copy-start(bf16[384]{0:T(512)(128)(2,1)} %param.38) | copy-start | bytes 2308
  12.8 73.2 %copy-start.9 = (bf16[1024,768]{1,0:T(8,128)(2,1)S(1)}, bf16[1024,768]{1,0:T(8,128)(2,1)}, u32[]{:S(2)}) copy-start(bf16[1024,768]{1,0:T(8,128)(2,1)} %param.26) | copy-start | bytes 4718596
  12.9 179.6 %copy-start.25 = (f32[1024]{0:T(1024)}, f32[1024]{0:T(1024)S(1)}, u32[]{:S(2)}) copy-start(f32[1024]{0:T(1024)S(1)} %fusion.76) | copy-start | bytes 12292
  26.0 76.0 %copy-start.27 = (f32[1024]{0:T(1024)}, f32[1024]{0:T(1024)S(1)}, u32[]{:S(2)}) copy-start(f32[1024]{0:T(1024)S(1)} %broadcast_multiply_fusion.1) | copy-start | bytes 12292
  39.3 33.8 %copy-start.41 = (f32[1024]{0:T(1024)}, f32[1024]{0:T(1024)S(1)}, u32[]{:S(2)}) copy-start(f32[1024]{0:T(1024)S(1)} %multiply_reduce_fusion.6) | copy-start | bytes 12292
  39.3 62.7 %copy-start.31 = (f32[1024]{0:T(1024)}, f32[1024]{0:T(1024)S(1)}, u32[]{:S(2)}) copy-start(f32[1024]{0:T(1024)S(1)} %fusion.86) | copy-start | bytes 12292
  73.1 28.9 %copy-start.29 = (f32[768]{0:T(1024)}, f32[768]{0:T(1024)S(1)}, u32[]{:S(2)}) copy-start(f32[768]{0:T(1024)S(1)} %convert_element_type.207) | copy-start | bytes 9220
  73.2 136.8 %copy-start.48 = (f32[768]{0:T(1024)}, f32[768]{0:T(1024)S(1)}, u32[]{:S(2)}) copy-start(f32[768]{0:T(1024)S(1)} %convert_element_type.219) | copy-start | bytes 9220
  192.4 15.4 %copy-start.8 = (bf16[6,1024,2,64]{1,3,2,0:T(8,128)(2,1)}, bf16[6,1024,2,64]{1,3,2,0:T(8,128)(2,1)S(1)}, u32[]{:S(2)}) copy-start(bf16[6,1024,2,64]{1,3,2,0:T(8,128)(2,1)S(1)} %get-tuple-element.453) | copy-start | bytes 4718596
  192.4 15.4 %copy-start.17 = (s32[6,1024]{1,0:T(8,128)}, s32[6,1024]{1,0:T(8,128)S(1)}, u32[]{:S(2)}) copy-start(s32[6,1024]{1,0:T(8,128)S(1)} %get-tuple-element.481) | copy-start | bytes 73732
  209.9 38.1 %copy-start.10 = (bf16[1024,768]{1,0:T(8,128)(2,1)S(1)}, bf16[1024,768]{1,0:T(8,128)(2,1)}, u32[]{:S(2)}) copy-start(bf16[1024,768]{1,0:T(8,128)(2,1)} %param.26) | copy-start | bytes 4718596
  290.9 276.1 %reduce-scatter.5.cloned.1.call-start = ((), (), s32[]{:S(2)}) async-start(), calls=%async_computation.8 | async-start | bytes 3981312 | tf_op jit(solution)/shard_map/reduce_scatter | solution.py:128
  438.0 129.1 %reduce-scatter.9.cloned.1.call-start = ((), (), s32[]{:S(2)}) async-start(), calls=%async_computation.10 | async-start | bytes 5308416 | tf_op jit(solution)/shard_map/reduce_scatter | solution.py:97
  448.6 143.7 %reduce-scatter.11.cloned.1.call-start = ((), (), s32[]{:S(2)}) async-start(), calls=%async_computation.11 | async-start | bytes 5308416 | tf_op jit(solution)/shard_map/reduce_scatter | solution.py:100
  459.9 198.6 %all-reduce.23.cloned.1.call-start = ((), (), s32[]{:S(2)}) async-start(), calls=%async_computation.12 | async-start | bytes 3538944 | tf_op jit(solution)/shard_map/psum | solution.py:151
  474.9 16.1 %copy-start.42 = (f32[1024]{0:T(1024)S(1)}, f32[1024]{0:T(1024)}, u32[]{:S(2)}) copy-start(f32[1024]{0:T(1024)} %copy-done.41) | copy-start | bytes 12292
  474.9 16.2 %copy-start.32 = (f32[1024]{0:T(1024)S(1)}, f32[1024]{0:T(1024)}, u32[]{:S(2)}) copy-start(f32[1024]{0:T(1024)} %copy-done.31) | copy-start | bytes 12292
  476.7 14.4 %copy-start.1 = (bf16[1024,768]{0,1:T(8,128)(2,1)S(1)}, bf16[1024,768]{0,1:T(8,128)(2,1)}, u32[]{:S(2)}) copy-start(bf16[1024,768]{0,1:T(8,128)(2,1)} %copy-done) | copy-start | bytes 4718596
  491.0 13.5 %copy-start.45 = (bf16[768]{0:T(1024)(128)(2,1)S(1)}, bf16[768]{0:T(1024)(128)(2,1)}, u32[]{:S(2)}) copy-start(bf16[768]{0:T(1024)(128)(2,1)} %get-tuple-element.240) | copy-start | bytes 4612
  491.0 13.5 %copy-start.46 = (bf16[768]{0:T(1024)(128)(2,1)S(1)}, bf16[768]{0:T(1024)(128)(2,1)}, u32[]{:S(2)}) copy-start(bf16[768]{0:T(1024)(128)(2,1)} %get-tuple-element.172) | copy-start | bytes 4612
  491.1 13.5 %copy-start.47 = (bf16[3072]{0:T(1024)(128)(2,1)S(1)}, bf16[3072]{0:T(1024)(128)(2,1)}, u32[]{:S(2)}) copy-start(bf16[3072]{0:T(1024)(128)(2,1)} %get-tuple-element.264) | copy-start | bytes 18436
  491.1 13.5 %copy-start.50 = (bf16[768]{0:T(1024)(128)(2,1)S(1)}, bf16[768]{0:T(1024)(128)(2,1)}, u32[]{:S(2)}) copy-start(bf16[768]{0:T(1024)(128)(2,1)} %get-tuple-element.262) | copy-start | bytes 4612
  491.1 56.9 %copy-start.34 = (f32[1024]{0:T(1024)S(1)}, f32[1024]{0:T(1024)}, u32[]{:S(2)}) copy-start(f32[1024]{0:T(1024)} %copy-done.33) | copy-start | bytes 12292
  564.3 28.0 %copy-start.4 = (f32[1024,768]{0,1:T(8,128)S(1)}, f32[1024,768]{0,1:T(8,128)}, u32[]{:S(2)}) copy-start(f32[1024,768]{0,1:T(8,128)} %copy-done.2) | copy-start | bytes 9437188
  658.5 5.4 copy-start.18
  (33 other events, 84.0 us)
Sparse Core Ops, SparseCore 0:
  9.7 44.2 all-gather.5
  55.6 21.6 all-gather.7
  78.9 50.9 all-gather.9
  131.4 50.2 all-gather.11
  291.0 31.4 reduce-scatter.6
  438.1 42.1 reduce-scatter.4
  482.6 54.0 reduce-scatter.8
  539.0 53.3 reduce-scatter.10
  595.8 62.6 all-reduce.22
where the time goes:
time: 682 us; the launch traced here: 672 us
  matrix products  291 us (43%)
  other arithmetic  146 us (21%)
  waiting for transfers between devices  82 us (12%)
  blocking collectives  81.7 us (12%)
  local copies, waits for them, and re-layouts  52.7 us (8%)
  between operations  17.4 us (3%)
    unnamed x2, blocking collectives  58.7 us
    psum x1, waiting for transfers between devices, reduce_attention(): lax.psum(shares[0].astype(jnp.bfloat16), 'narrow').astype(jnp.float32)  54 us
    dot_general x1, matrix products, per_device(): jnp.dot(normed_two_low, full_up, preferred_element_type=jnp.float32)  38.1 us
    reduce_sum x3, other arithmetic, layer_norm(): return center * lax.rsqrt(spread + 1e-06) * gain + shift  31.2 us
    dot_general x12, matrix products, masked_scores(): jnp.einsum('qhd,khd->hqk', queries, key_rows, preferred_element_type=jnp....  31 us
    dot_general x6, matrix products, pair_forward(): jnp.einsum('hqk,khd->qhd', probabilities.astype(jnp.bfloat16), values, pr...  26.4 us
    reduce_scatter x1, waiting for transfers between devices, reduce_feedforward(): lax.psum_scatter(gradients[1].astype(jnp.bfloat16), 'wide', scatter_dimen...  25.3 us
    dot_general x6, matrix products, pair_backward(): jnp.einsum('qhd,khd->hqk', grad_out, values, preferred_element_type=jnp.f...  25 us
  transfers between devices with their start and end apart: 9, of which 2 were waited for; matrix products, arithmetic and copies ran while one was open for 64% of the time, Pallas kernels for 0%

commit v1 on v0

--- a/solution.py
+++ b/solution.py
@@ -148,7 +148,9 @@
         ).astype(jnp.float32),
     )
     return (
-        lax.psum(shares[0].astype(jnp.bfloat16), "narrow").astype(jnp.float32),
+        jnp.sum(lax.all_gather(shares[0].astype(jnp.bfloat16), "narrow"), axis=0).astype(
+            jnp.float32
+        ),
         lax.psum(shares[1].astype(jnp.bfloat16), "narrow").astype(jnp.float32),
         lax.psum(shares[2].astype(jnp.bfloat16), "narrow").astype(jnp.float32),
         lax.psum(shares[3].astype(jnp.bfloat16), "narrow").astype(jnp.float32),

time: 682 us -> 723 us (1.060)
  waiting for transfers between devices: 82 us -> 138 us
  local copies, waits for them, and re-layouts: 52.7 us -> 43.6 us
    reduce_scatter x1, waiting for transfers between devices: 25.3 us -> 50.7 us  [reduce_feedforward(): lax.psum_scatter(gradients[1].astype(jnp.bfloat16), 'wide', scatter_dimen...]
    all_gather x0 -> x1, waiting for transfers between devices: none -> 20.7 us  [reduce_attention(): lax.all_gather(shares[0].astype(jnp.bfloat16), 'narrow')]
    unnamed x151 -> x149, local copies, waits for them, and re-layouts: 17.4 us -> 16.3 us
  transfers between devices with their start and end apart: 9 -> 10, of which waited for: 2 -> 4; matrix products, arithmetic and copies ran while one was open for 64% -> 41% of each run, Pallas kernels for 0% -> 0%
where the time goes in v1:
time: 723 us; the launch traced here: 713 us
  matrix products  290 us (40%)
  other arithmetic  142 us (20%)
  waiting for transfers between devices  138 us (19%)
  blocking collectives  81.3 us (11%)
  local copies, waits for them, and re-layouts  43.6 us (6%)
  between operations  17.5 us (2%)
    unnamed x2, blocking collectives  58.6 us
    psum x1, waiting for transfers between devices, reduce_attention(): lax.psum(shares[1].astype(jnp.bfloat16), 'narrow').astype(jnp.float32)  57.6 us
    reduce_scatter x1, waiting for transfers between devices, reduce_feedforward(): lax.psum_scatter(gradients[1].astype(jnp.bfloat16), 'wide', scatter_dimen...  50.7 us
    dot_general x1, matrix products, per_device(): jnp.dot(normed_two_low, full_up, preferred_element_type=jnp.float32)  38.1 us
    reduce_sum x3, other arithmetic, layer_norm(): return center * lax.rsqrt(spread + 1e-06) * gain + shift  31.2 us
    dot_general x12, matrix products, masked_scores(): jnp.einsum('qhd,khd->hqk', queries, key_rows, preferred_element_type=jnp....  31 us
    dot_general x6, matrix products, pair_forward(): jnp.einsum('hqk,khd->qhd', probabilities.astype(jnp.bfloat16), values, pr...  26.4 us
    dot_general x6, matrix products, pair_backward(): jnp.einsum('qhd,khd->hqk', grad_out, values, preferred_element_type=jnp.f...  25.1 us
  transfers between devices with their start and end apart: 10, of which 4 were waited for; matrix products, arithmetic and copies ran while one was open for 41% of the time, Pallas kernels for 0%

profile of v1, /device:TPU:0, one launch (start us, length us, event | category | flops | bytes accessed | tf_op | source)
XLA Modules:
  0.0 713.3 jit_solution(12938708907230480839)
XLA Ops:
  12.9 13.1 %fusion.92 = f32[1024]{0:T(1024)S(1)} fusion(f32[768]{0:T(1024)S(1)} %fusion.71, f32[1024]{0:T(1024)S(1)} %get-tuple-element.253, f32[1024]{0:T(1024)S(1)} %get-tuple-element.252, pred[768]{0:T(1024)(128)(4,1)S(1)} %get-tuple-element.266, f32[1024]{0:T(1024)S(1)} %fusion.76, pred[768]{0:T(1024)(128)(4,1)S(1)} %fusion.81, ...), kind=kLoop, calls=%fused_computation.165 | loop fusion | flops 5504000 | bytes 1594624 | tf_op jit(solution)/shard_map/reduce_sum | solution.py:14
  26.0 13.3 %multiply_reduce_fusion.6 = f32[1024]{0:T(1024)S(1)} fusion(f32[1024]{0:T(1024)S(1)} %broadcast_multiply_fusion.1, f32[768]{0:T(1024)S(1)} %fusion.71, f32[1024]{0:T(1024)S(1)} %get-tuple-element.253, f32[1024]{0:T(1024)S(1)} %get-tuple-element.252, pred[768]{0:T(1024)(128)(4,1)S(1)} %get-tuple-element.266, f32[1024]{0:T(1024)S(1)} %fusion.76, ...), kind=kLoop, calls=%fused_computation.97 | loop fusion | flops 7076864 | bytes 1598720 | tf_op jit(solution)/shard_map/reduce_sum | solution.py:15
  42.3 30.8 %all-reduce.18 = (bf16[768]{0:T(1024)(128)(2,1)S(1)}, bf16[768]{0:T(1024)(128)(2,1)S(1)}, bf16[768]{0:T(1024)(128)(2,1)S(1)}, bf16[768]{0:T(1024)(128)(2,1)S(1)}...) all-reduce(bf16[768]{0:T(1024)(128)(2,1)S(1)} %dynamic-update-slice, ...), channel_id=1, replica_groups=mesh['narrow'=4,'wide'=8] {'wide'}, use_global_device_ids=true, to_apply=%add.3 | all-reduce | flops 5376 | bytes 21504
  73.2 12.8 %all-gather.1 = bf16[8,1,384]{2,1,0:T(2,128)(2,1)S(1)} all-gather(bf16[1,1,384]{2,1,0:T(2,128)(2,1)S(1)} %reshape.409), channel_id=1, replica_groups=mesh['narrow'=4,'wide'=8] {'wide'}, dimensions={0}, use_global_device_ids=true | all-gather | bytes 6912 | tf_op jit(solution)/shard_map/all_gather | solution.py:240
  87.7 14.2 %add_convert_fusion.13 = bf16[1024,768]{0,1:T(8,128)(2,1)} fusion(f32[768]{0:T(1024)S(1)} %convert_element_type.210, f32[768]{0:T(1024)S(1)} %convert_element_type.209, f32[1024]{0:T(1024)S(1)} %fusion.86, f32[1024]{0:T(1024)S(1)} %broadcast_multiply_fusion.1, f32[768]{0:T(1024)S(1)} %fusion.71, f32[1024]{0:T(1024)S(1)} %get-tuple-element.253, ...), kind=kLoop, calls=%fused_computation.96.clone.clone.2 | loop fusion | flops 8650752 | bytes 3177728 | tf_op jit(solution)/shard_map/rd,re->de/dot_general | solution.py:320
  101.9 17.8 %add_convert_fusion.1 = bf16[1024,2304]{1,0:T(8,128)(2,1)S(1)} fusion(bf16[768,2304]{1,0:T(8,128)(2,1)} %all-gather.8.cloned.1.call-done, f32[2304]{0:T(1024)S(1)} %pad_maximum_fusion.3, f32[768]{0:T(1024)S(1)} %convert_element_type.210, f32[768]{0:T(1024)S(1)} %convert_element_type.209, f32[1024]{0:T(1024)S(1)} %fusion.86, ...), kind=kOutput, calls=%fused_computation.79 | convolution fusion | flops 3637248000 | bytes 9871616 | tf_op jit(solution)/shard_map/dot_general | solution.py:218
  129.0 59.7 %while.26 = (s32[]{:T(128)}, bf16[6,1024,2,64]{1,3,2,0:T(8,128)(2,1)}, f32[6,2,1024]{2,1,0:T(2,128)S(1)}, bf16[6,1024,2,64]{1,3,2,0:T(8,128)(2,1)}, s32[6,1024]{...) while((s32[]{:T(128)}, ...), condition=%wide.region_6.7_spmd, body=%wide.region_3.6_spmd.sunk | while | flops 563083264 | bytes 30750812 | solution.py:226
  134.5 4.4 fusion.143
  144.5 4.4 fusion.143
  154.4 4.4 fusion.143
  164.4 4.4 fusion.143
  174.3 4.4 fusion.143
  184.3 4.4 fusion.143
  188.8 15.3 %fusion.99 = (f32[1024]{0:T(1024)S(1)}, f32[1024,768]{0,1:T(8,128)S(1)}) fusion(f32[768]{0:T(1024)S(1)} %convert_element_type.219, bf16[1024,768]{0,1:T(8,128)(2,1)} %bitcast.32, bf16[768,768]{1,0:T(8,128)(2,1)} %all-gather.10.cloned.1.call-done, f32[768]{0:T(1024)S(1)} %fusion.71, f32[1024]{0:T(1024)S(1)} %get-tuple-element.253, ...), kind=kOutput, calls=%fused_computation.170 | convolution fusion | flops 1215036416 | bytes 7495936 | tf_op jit(solution)/shard_map/dot_general | solution.py:232
  206.2 38.1 %multiply_convert_fusion.1 = (bf16[1024,3072]{1,0:T(8,128)(2,1)}, f32[1024,3072]{1,0:T(8,128)}, f32[1024,3072]{1,0:T(8,128)}) fusion(f32[3072]{0:T(1024)S(1)} %bitcast.184, bf16[768,3072]{1,0:T(8,128)(2,1)} %all-gather.12.cloned.1.call-done, f32[1024,768]{0,1:T(8,128)} %copy-done.2, f32[768]{0:T(1024)S(1)} %convert_element_type.221, ...), kind=kOutput, calls=%fused_computation.65 | convolution fusion | flops 5043388416 | bytes 39348224 | tf_op jit(solution)/shard_map/dot_general | solution.py:247
  244.3 17.4 %fusion.102 = (bf16[3072]{0:T(1024)(128)(2,1)}, bf16[1024,3072]{1,0:T(8,128)(2,1)}) fusion(f32[1024,3072]{1,0:T(8,128)} %get-tuple-element.244, bf16[1024,768]{1,0:T(8,128)(2,1)S(1)} %copy-done.10, bf16[3072,768]{1,0:T(8,128)(2,1)} %all-gather.14.cloned.1.call-done, f32[1024,3072]{1,0:T(8,128)} %get-tuple-element.258, f32[3072]{0:T(1024)S(1)} %bitcast.185), kind=kOutput, calls=%fused_computation.173 | convolution fusion | flops 4882166784 | bytes 37767168 | tf_op jit(solution)/shard_map/rd,fd->rf/dot_general | solution.py:267
  261.7 10.7 %fusion.101 = (bf16[768]{0:T(1024)(128)(2,1)}, f32[1024,768]{1,0:T(8,128)}) fusion(bf16[1024,3072]{1,0:T(8,128)(2,1)} %get-tuple-element.264, bf16[768,3072]{1,0:T(8,128)(2,1)} %all-gather.12.cloned.1.call-done), kind=kOutput, calls=%fused_computation.172 | convolution fusion | flops 4832623616 | bytes 14157312 | tf_op jit(solution)/shard_map/rf,df->rd/dot_general | solution.py:274
  272.4 3.7 copy.91
  276.0 3.5 multiply_reduce_fusion.1
  289.6 121.9 %while.27 = (s32[]{:T(128)}, bf16[6,1024,2,64]{1,3,2,0:T(8,128)(2,1)}, bf16[6,1024,2,64]{1,3,2,0:T(8,128)(2,1)}, bf16[6,1024,2,64]{1,3,2,0:T(8,128)(2,1)}, bf16[...) while((s32[]{:T(128)}, ...), condition=%wide.region_13.14_spmd, body=%wide.region_11.13_spmd.sunk | while | flops 1374943232 | bytes 83174576 | solution.py:307
  292.6 4.2 multiply_reduce_fusion.8
  299.5 3.2 fusion.154
  305.7 4.2 fusion.155
  312.9 4.2 multiply_reduce_fusion.8
  326.1 4.2 fusion.155
  333.3 4.2 multiply_reduce_fusion.8
  346.4 4.2 fusion.155
  353.6 4.2 multiply_reduce_fusion.8
  366.7 4.2 fusion.155
  373.9 4.2 multiply_reduce_fusion.8
  387.0 4.2 fusion.155
  394.2 4.2 multiply_reduce_fusion.8
  407.3 4.1 fusion.155
  411.5 8.4 %convolution_convert_fusion.2 = bf16[768,2304]{1,0:T(8,128)(2,1)} fusion(bf16[1024,768]{0,1:T(8,128)(2,1)} %bitcast.51, bf16[1024,768]{0,1:T(8,128)(2,1)} %bitcast.179, bf16[1024,768]{0,1:T(8,128)(2,1)} %bitcast.175, bf16[1024,768]{0,1:T(8,128)(2,1)} %add_convert_fusion.13), kind=kOutput, calls=%fused_computation.82 | convolution fusion | flops 3639803904 | bytes 9830400 | tf_op jit(solution)/shard_map/rd,re->de/dot_general | solution.py:320
  420.2 4.3 convolution_convert_fusion.4
  424.6 9.8 %convolution_convert_fusion.1 = bf16[768,3072]{1,0:T(8,128)(2,1)} fusion(bf16[1024,3072]{1,0:T(8,128)(2,1)} %get-tuple-element.264, f32[1024,768]{0,1:T(8,128)S(1)} %copy-done.3, f32[768]{0:T(1024)S(1)} %copy-done.47, f32[768]{0:T(1024)S(1)} %convert_element_type.220, f32[1024]{0:T(1024)S(1)} %fusion.87, f32[1024]{0:T(1024)S(1)} %broadcast_multiply_fusion), kind=kOutput, calls=%fused_computation.81 | convolution fusion | flops 4838129664 | bytes 14170112 | tf_op jit(solution)/shard_map/rd,rf->df/dot_general | solution.py:271
  435.8 9.8 %convolution_convert_fusion = bf16[3072,768]{1,0:T(8,128)(2,1)} fusion(bf16[1024,3072]{1,0:T(8,128)(2,1)} %get-tuple-element.243, bf16[1024,768]{1,0:T(8,128)(2,1)S(1)} %copy-done.11), kind=kOutput, calls=%fused_computation.80 | convolution fusion | flops 4834197504 | bytes 12582912 | tf_op jit(solution)/shard_map/rf,rd->fd/dot_general | solution.py:264
  447.7 8.7 %fusion.100 = (bf16[768]{0:T(1024)(128)(2,1)S(1)}, f32[1024,768]{1,0:T(8,128)}) fusion(bf16[768,2304]{1,0:T(8,128)(2,1)} %all-gather.8.cloned.1.call-done, bf16[1024,768]{0,1:T(8,128)(2,1)} %bitcast.51, bf16[1024,768]{0,1:T(8,128)(2,1)} %bitcast.180, bf16[1024,768]{0,1:T(8,128)(2,1)S(1)} %bitcast.176), kind=kOutput, calls=%fused_computation.171 | convolution fusion | flops 3638820096 | bytes 11404800 | tf_op jit(solution)/shard_map/re,de->rd/dot_general | solution.py:323
  456.4 5.9 reduce-scatter.5.cloned.1.call-done
  467.3 14.3 %multiply_reduce_fusion.3 = f32[1024]{0:T(1024)S(1)} fusion(f32[1024,768]{0,1:T(8,128)S(1)} %copy.92, f32[768]{0:T(1024)S(1)} %copy-done.28, f32[1024]{0:T(1024)S(1)} %copy-done.26, f32[768]{0:T(1024)S(1)} %copy-done.18, f32[1024]{0:T(1024)S(1)} %copy-done.22, f32[1024]{0:T(1024)S(1)} %copy-done.20, pred[768]{0:T(1024)(128)(4,1)S(1)} %copy-done.36, ...), kind=kLoop, calls=%fused_computation.89 | loop fusion | flops 7863296 | bytes 4747520 | tf_op jit(solution)/shard_map/transpose(jvp())/reduce_sum | solution.py:16
  481.6 13.4 %multiply_reduce_fusion.2 = (bf16[768]{0:T(1024)(128)(2,1)S(1)}, f32[1024]{0:T(1024)S(1)}) fusion(f32[1024,768]{0,1:T(8,128)S(1)} %copy.92, f32[1024]{0:T(1024)S(1)} %copy-done.30, f32[1024]{0:T(1024)S(1)} %copy-done.26, f32[768]{0:T(1024)S(1)} %copy-done.18, f32[1024]{0:T(1024)S(1)} %copy-done.22, f32[1024]{0:T(1024)S(1)} %copy-done.20, ...), kind=kLoop, calls=%fused_computation.87 | loop fusion | flops 12581120 | bytes 4757248 | tf_op jit(solution)/shard_map/transpose(jvp())/reduce_sum | solution.py:16
  495.1 27.8 %all-reduce.17 = (bf16[768]{0:T(1024)(128)(2,1)S(1)}, bf16[768]{0:T(1024)(128)(2,1)S(1)}, bf16[768]{0:T(1024)(128)(2,1)S(1)}, bf16[768]{0:T(1024)(128)(2,1)S(1)}...) all-reduce(bf16[768]{0:T(1024)(128)(2,1)S(1)} %dynamic-update-slice, ...), channel_id=1, replica_groups=mesh['narrow'=4,'wide'=8] {'wide'}, use_global_device_ids=true, to_apply=%add.7 | all-reduce | flops 9984 | bytes 39936
  523.5 10.0 %all-reduce.19 = (bf16[96]{0:T(256)(128)(2,1)S(1)}, bf16[96]{0:T(256)(128)(2,1)S(1)}, bf16[96]{0:T(256)(128)(2,1)S(1)}, bf16[96]{0:T(256)(128)(2,1)S(1)}, bf16[9...) all-reduce(bf16[96]{0:T(256)(128)(2,1)S(1)} %dynamic-slice.9, ...), channel_id=1, replica_groups=mesh['narrow'=4,'wide'=8] {'narrow'}, use_global_device_ids=true, to_apply=%region_26.27 | all-reduce | flops 1152 | bytes 4608 | tf_op jit(solution)/shard_map/psum | solution.py:155
  538.2 16.3 %add_convert_fusion.2 = bf16[1024,768]{0,1:T(8,128)(2,1)} fusion(f32[1024,768]{0,1:T(8,128)} %copy-done.6, bf16[1024,768]{0,1:T(8,128)(2,1)} %copy.90, f32[1024]{0:T(1024)S(1)} %negate_multiply_fusion.1, f32[1024]{0:T(1024)S(1)} %copy-done.32, f32[1024]{0:T(1024)S(1)} %multiply_multiply_fusion.5, f32[1024]{0:T(1024)S(1)} %copy-done.26, ...), kind=kLoop, calls=%fused_computation.88 | loop fusion | flops 14155776 | bytes 11051264 | tf_op jit(solution)/shard_map/convert_element_type | solution.py:329
  557.2 50.7 %reduce-scatter.11.cloned.1.call-done = bf16[384,768]{1,0:T(8,128)(2,1)} async-done(((bf16[3072,768]{1,0:T(8,128)(2,1)}), bf16[384,768]{1,0:T(8,128)(2,1)}) %reduce-scatter.11.cloned.1.call-update) | async-done | bytes 589840 | tf_op jit(solution)/shard_map/reduce_scatter | solution.py:100
  608.0 9.5 %add_convert_fusion.3 = bf16[1024,768]{0,1:T(8,128)(2,1)} fusion(f32[1024,768]{0,1:T(8,128)S(1)} %copy-done.4, bf16[1024,3072]{1,0:T(8,128)(2,1)} %get-tuple-element.243, bf16[3072,768]{1,0:T(8,128)(2,1)} %all-gather.14.cloned.1.call-done, f32[768]{0:T(1024)S(1)} %convert_element_type.225), kind=kOutput, calls=%fused_computation.92 | convolution fusion | flops 4834197504 | bytes 15731712 | tf_op jit(solution)/shard_map/dot_general | solution.py:254
  620.1 20.7 %all-gather.16.cloned.1.call-done = bf16[384,2304]{1,0:T(8,128)(2,1)} async-done(((bf16[96,2304]{1,0:T(8,128)(2,1)}), bf16[384,2304]{1,0:T(8,128)(2,1)}) %all-gather.16.cloned.1.call-update) | async-done | bytes 1769488 | tf_op jit(solution)/shard_map/all_gather | solution.py:151
  643.6 57.6 %all-reduce.23.cloned.1.call-done = (bf16[96,768]{1,0:T(8,128)(2,1)}, bf16[96,3072]{1,0:T(8,128)(2,1)}, bf16[384,768]{1,0:T(8,128)(2,1)}) async-done(((bf16[96,768]{1,0:T(8,128)(2,1)}, bf16[96,3072]{1,0:T(8,128)(2,1)}, bf16[384,768]{1,0:T(8,128)(2,1)}), (bf16[96,768]{1,0:T(8,128)(2,1)}, bf16[96,3072]{1,0:T(8,128)(2,1)}, bf16[384,768]{1,0:T(8,128)(2,1)})) %all-reduce.23.cloned.1.call-update) | async-done | bytes 1327120 | tf_op jit(solution)/shard_map/psum | solution.py:154
  (329 shorter events, 157.9 us)
Async XLA Ops:
  7.2 5.7 copy-start.37
  7.2 5.6 copy-start.51
  7.2 5.6 copy-start.38
  7.2 94.7 %all-gather.8.cloned.1.call-start = ((), (), s32[]{:S(2)}) async-start(), calls=%async_computation.4 | async-start | bytes 3981312 | tf_op jit(solution)/shard_map/all_gather | solution.py:201
  7.9 180.8 %all-gather.10.cloned.1.call-start = ((), (), s32[]{:S(2)}) async-start(), calls=%async_computation.5 | async-start | bytes 1327104 | tf_op jit(solution)/shard_map/all_gather | solution.py:202
  8.7 197.5 %all-gather.12.cloned.1.call-start = ((), (), s32[]{:S(2)}) async-start(), calls=%async_computation.6 | async-start | bytes 5308416 | tf_op jit(solution)/shard_map/all_gather | solution.py:236
  9.4 234.8 %all-gather.14.cloned.1.call-start = ((), (), s32[]{:S(2)}) async-start(), calls=%async_computation.7 | async-start | bytes 5308416 | tf_op jit(solution)/shard_map/all_gather | solution.py:237
  10.0 452.2 %reduce-scatter.5.cloned.1.call-start = ((), (), s32[]{:S(2)}) async-start(), calls=%async_computation.8 | async-start | bytes 3981312 | tf_op jit(solution)/shard_map/reduce_scatter | solution.py:128
  10.1 178.6 %copy-start.33 = (pred[768]{0:T(1024)(128)(4,1)}, pred[768]{0:T(1024)(128)(4,1)S(1)}, u32[]{:S(2)}) copy-start(pred[768]{0:T(1024)(128)(4,1)S(1)} %get-tuple-element.265) | copy-start | bytes 2308
  10.1 178.6 %copy-start.35 = (pred[768]{0:T(1024)(128)(4,1)}, pred[768]{0:T(1024)(128)(4,1)S(1)}, u32[]{:S(2)}) copy-start(pred[768]{0:T(1024)(128)(4,1)S(1)} %get-tuple-element.266) | copy-start | bytes 2308
  10.1 178.6 %copy-start.17 = (f32[768]{0:T(1024)}, f32[768]{0:T(1024)S(1)}, u32[]{:S(2)}) copy-start(f32[768]{0:T(1024)S(1)} %fusion.71) | copy-start | bytes 9220
  10.1 178.6 %copy-start.41 = (pred[768]{0:T(1024)(128)(4,1)}, pred[768]{0:T(1024)(128)(4,1)S(1)}, u32[]{:S(2)}) copy-start(pred[768]{0:T(1024)(128)(4,1)S(1)} %fusion.81) | copy-start | bytes 2308
  10.9 177.9 %copy-start.19 = (f32[1024]{0:T(1024)}, f32[1024]{0:T(1024)S(1)}, u32[]{:S(2)}) copy-start(f32[1024]{0:T(1024)S(1)} %get-tuple-element.252) | copy-start | bytes 12292
  10.9 177.9 %copy-start.21 = (f32[1024]{0:T(1024)}, f32[1024]{0:T(1024)S(1)}, u32[]{:S(2)}) copy-start(f32[1024]{0:T(1024)S(1)} %get-tuple-element.253) | copy-start | bytes 12292
  12.6 176.1 %copy-start = (bf16[1024,768]{0,1:T(8,128)(2,1)}, bf16[1024,768]{0,1:T(8,128)(2,1)S(1)}, u32[]{:S(2)}) copy-start(bf16[1024,768]{0,1:T(8,128)(2,1)S(1)} %copy.85) | copy-start | bytes 4718596
  12.6 26.7 %copy-start.49 = (u32[32]{0:T(128)S(1)}, u32[32]{0:T(128)}, u32[]{:S(2)}) copy-start(u32[32]{0:T(128)} %constant.212) | copy-start | bytes 388
  12.7 28.0 %copy-start.53 = (bf16[96]{0:T(256)(128)(2,1)S(1)}, bf16[96]{0:T(256)(128)(2,1)}, u32[]{:S(2)}) copy-start(bf16[96]{0:T(256)(128)(2,1)} %param.31) | copy-start | bytes 580
  12.7 28.2 %copy-start.54 = (bf16[96]{0:T(256)(128)(2,1)S(1)}, bf16[96]{0:T(256)(128)(2,1)}, u32[]{:S(2)}) copy-start(bf16[96]{0:T(256)(128)(2,1)} %param.32) | copy-start | bytes 580
  12.7 28.4 %copy-start.55 = (bf16[96]{0:T(256)(128)(2,1)S(1)}, bf16[96]{0:T(256)(128)(2,1)}, u32[]{:S(2)}) copy-start(bf16[96]{0:T(256)(128)(2,1)} %param.33) | copy-start | bytes 580
  12.7 28.6 %copy-start.56 = (bf16[96]{0:T(256)(128)(2,1)S(1)}, bf16[96]{0:T(256)(128)(2,1)}, u32[]{:S(2)}) copy-start(bf16[96]{0:T(256)(128)(2,1)} %param.34) | copy-start | bytes 580
  12.7 28.9 %copy-start.57 = (bf16[96]{0:T(256)(128)(2,1)S(1)}, bf16[96]{0:T(256)(128)(2,1)}, u32[]{:S(2)}) copy-start(bf16[96]{0:T(256)(128)(2,1)} %param.35) | copy-start | bytes 580
  12.7 29.1 %copy-start.58 = (bf16[96]{0:T(256)(128)(2,1)S(1)}, bf16[96]{0:T(256)(128)(2,1)}, u32[]{:S(2)}) copy-start(bf16[96]{0:T(256)(128)(2,1)} %param.36) | copy-start | bytes 580
  12.7 29.3 %copy-start.59 = (bf16[96]{0:T(256)(128)(2,1)S(1)}, bf16[96]{0:T(256)(128)(2,1)}, u32[]{:S(2)}) copy-start(bf16[96]{0:T(256)(128)(2,1)} %param.37) | copy-start | bytes 580
  12.7 60.4 %copy-start.50 = (bf16[384]{0:T(512)(128)(2,1)S(1)}, bf16[384]{0:T(512)(128)(2,1)}, u32[]{:S(2)}) copy-start(bf16[384]{0:T(512)(128)(2,1)} %param.38) | copy-start | bytes 2308
  12.8 73.2 %copy-start.9 = (bf16[1024,768]{1,0:T(8,128)(2,1)S(1)}, bf16[1024,768]{1,0:T(8,128)(2,1)}, u32[]{:S(2)}) copy-start(bf16[1024,768]{1,0:T(8,128)(2,1)} %param.26) | copy-start | bytes 4718596
  12.9 175.9 %copy-start.23 = (f32[1024]{0:T(1024)}, f32[1024]{0:T(1024)S(1)}, u32[]{:S(2)}) copy-start(f32[1024]{0:T(1024)S(1)} %fusion.76) | copy-start | bytes 12292
  26.0 75.9 %copy-start.25 = (f32[1024]{0:T(1024)}, f32[1024]{0:T(1024)S(1)}, u32[]{:S(2)}) copy-start(f32[1024]{0:T(1024)S(1)} %broadcast_multiply_fusion.1) | copy-start | bytes 12292
  39.3 33.8 %copy-start.39 = (f32[1024]{0:T(1024)}, f32[1024]{0:T(1024)S(1)}, u32[]{:S(2)}) copy-start(f32[1024]{0:T(1024)S(1)} %multiply_reduce_fusion.6) | copy-start | bytes 12292
  39.3 62.6 %copy-start.29 = (f32[1024]{0:T(1024)}, f32[1024]{0:T(1024)S(1)}, u32[]{:S(2)}) copy-start(f32[1024]{0:T(1024)S(1)} %fusion.86) | copy-start | bytes 12292
  73.1 28.8 %copy-start.27 = (f32[768]{0:T(1024)}, f32[768]{0:T(1024)S(1)}, u32[]{:S(2)}) copy-start(f32[768]{0:T(1024)S(1)} %convert_element_type.209) | copy-start | bytes 9220
  73.2 133.0 %copy-start.46 = (f32[768]{0:T(1024)}, f32[768]{0:T(1024)S(1)}, u32[]{:S(2)}) copy-start(f32[768]{0:T(1024)S(1)} %convert_element_type.221) | copy-start | bytes 9220
  188.7 15.3 %copy-start.8 = (bf16[6,1024,2,64]{1,3,2,0:T(8,128)(2,1)}, bf16[6,1024,2,64]{1,3,2,0:T(8,128)(2,1)S(1)}, u32[]{:S(2)}) copy-start(bf16[6,1024,2,64]{1,3,2,0:T(8,128)(2,1)S(1)} %get-tuple-element.451) | copy-start | bytes 4718596
  206.2 38.1 %copy-start.10 = (bf16[1024,768]{1,0:T(8,128)(2,1)S(1)}, bf16[1024,768]{1,0:T(8,128)(2,1)}, u32[]{:S(2)}) copy-start(bf16[1024,768]{1,0:T(8,128)(2,1)} %param.26) | copy-start | bytes 4718596
  419.9 4.6 copy-start.47
  420.0 137.3 %reduce-scatter.7.cloned.1.call-start = ((), (), s32[]{:S(2)}) async-start(), calls=%async_computation.9 | async-start | bytes 1327104 | tf_op jit(solution)/shard_map/reduce_scatter | solution.py:131
  424.5 132.7 %reduce-scatter.9.cloned.1.call-start = ((), (), s32[]{:S(2)}) async-start(), calls=%async_computation.10 | async-start | bytes 5308416 | tf_op jit(solution)/shard_map/reduce_scatter | solution.py:97
  434.4 173.6 %reduce-scatter.11.cloned.1.call-start = ((), (), s32[]{:S(2)}) async-start(), calls=%async_computation.11 | async-start | bytes 5308416 | tf_op jit(solution)/shard_map/reduce_scatter | solution.py:100
  445.7 195.1 %all-gather.16.cloned.1.call-start = ((), (), s32[]{:S(2)}) async-start(), calls=%async_computation.12 | async-start | bytes 2211840 | tf_op jit(solution)/shard_map/all_gather | solution.py:151
  462.3 238.9 %all-reduce.23.cloned.1.call-start = ((), (), s32[]{:S(2)}) async-start(), calls=%async_computation.13 | async-start | bytes 2654208 | tf_op jit(solution)/shard_map/psum | solution.py:154
  465.4 16.2 %copy-start.40 = (f32[1024]{0:T(1024)S(1)}, f32[1024]{0:T(1024)}, u32[]{:S(2)}) copy-start(f32[1024]{0:T(1024)} %copy-done.39) | copy-start | bytes 12292
  465.4 16.2 %copy-start.30 = (f32[1024]{0:T(1024)S(1)}, f32[1024]{0:T(1024)}, u32[]{:S(2)}) copy-start(f32[1024]{0:T(1024)} %copy-done.29) | copy-start | bytes 12292
  467.2 14.4 %copy-start.1 = (bf16[1024,768]{0,1:T(8,128)(2,1)S(1)}, bf16[1024,768]{0,1:T(8,128)(2,1)}, u32[]{:S(2)}) copy-start(bf16[1024,768]{0,1:T(8,128)(2,1)} %copy-done) | copy-start | bytes 4718596
  481.5 13.5 %copy-start.43 = (bf16[768]{0:T(1024)(128)(2,1)S(1)}, bf16[768]{0:T(1024)(128)(2,1)}, u32[]{:S(2)}) copy-start(bf16[768]{0:T(1024)(128)(2,1)} %get-tuple-element.239) | copy-start | bytes 4612
  481.6 13.5 %copy-start.44 = (bf16[768]{0:T(1024)(128)(2,1)S(1)}, bf16[768]{0:T(1024)(128)(2,1)}, u32[]{:S(2)}) copy-start(bf16[768]{0:T(1024)(128)(2,1)} %get-tuple-element.172) | copy-start | bytes 4612
  481.6 13.5 %copy-start.45 = (bf16[3072]{0:T(1024)(128)(2,1)S(1)}, bf16[3072]{0:T(1024)(128)(2,1)}, u32[]{:S(2)}) copy-start(bf16[3072]{0:T(1024)(128)(2,1)} %get-tuple-element.263) | copy-start | bytes 18436
  481.6 13.5 %copy-start.48 = (bf16[768]{0:T(1024)(128)(2,1)S(1)}, bf16[768]{0:T(1024)(128)(2,1)}, u32[]{:S(2)}) copy-start(bf16[768]{0:T(1024)(128)(2,1)} %get-tuple-element.261) | copy-start | bytes 4612
  481.6 56.6 %copy-start.32 = (f32[1024]{0:T(1024)S(1)}, f32[1024]{0:T(1024)}, u32[]{:S(2)}) copy-start(f32[1024]{0:T(1024)} %copy-done.31) | copy-start | bytes 12292
  554.5 53.5 %copy-start.4 = (f32[1024,768]{0,1:T(8,128)S(1)}, f32[1024,768]{0,1:T(8,128)}, u32[]{:S(2)}) copy-start(f32[1024,768]{0,1:T(8,128)} %copy-done.2) | copy-start | bytes 9437188
  (33 other events, 94.0 us)
Sparse Core Ops, SparseCore 0:
  9.7 44.2 all-gather.7
  55.6 21.6 all-gather.9
  78.9 50.9 all-gather.11
  131.4 49.9 all-gather.13
  420.1 42.1 reduce-scatter.4
  465.0 31.5 reduce-scatter.6
  498.9 53.3 reduce-scatter.8
  554.6 53.3 reduce-scatter.10
  609.8 30.9 all-gather.15
  644.0 57.0 all-reduce.22
